TPU v7x, 1024 devices: a whole 4x8x16 slice. The times are simulated.
1024 devices in a mesh: wide: 64 (over x, y, core), narrow: 16 (over z).
Axes of the slice: x: 4, y: 8, z: 16, core: 2. Of those that a mesh axis runs over, the one named last changes fastest.
Arguments:
- tokens: bfloat16 [1536, 4096], P('wide', 'narrow'), may hold values from -6 to 6
- grad_out: bfloat16 [1536, 4096], P('wide', 'narrow'), may hold values from -1.1953125 to 1.1953125
- expert_ids: int32 [1536, 8], P('wide'), may hold values from 0 to 63, all different within a row; in each aligned block of 24 rows (0 to 23, 24 to 47, ...) at most 6 rows name the same one
- route_weights: bfloat16 [1536, 8], P('wide'), may hold values from 0.049804688 to 1
- w_gate: bfloat16 [64, 4096, 1536], P('wide', None, 'narrow'), may hold values from -0.09375 to 0.09375
- w_up: bfloat16 [64, 4096, 1536], P('wide', None, 'narrow'), may hold values from -0.09375 to 0.09375
- w_down: bfloat16 [64, 1536, 4096], P('wide', 'narrow'), may hold values from -0.15625 to 0.15625
Outputs:
- grad_tokens: bfloat16 [1536, 4096], P('wide', 'narrow')
- grad_route: bfloat16 [1536, 8], P('wide')
- grad_down: bfloat16 [64, 1536, 4096], P('wide', 'narrow')
Inputs may be any that keep to these rules, and one draw needn't show every extreme that they name: `expert_ids`: each row names 8 different experts. In each aligned block of 24 rows (the tokens of one index of wide) no expert is named by more than 6 rows, a bound that some block reaches.
All inputs are finite; a program needn't handle non-finite values.
Results may differ from a plain program's by a relative error of at most 0.019.
Values may be sent and summed in bfloat16 or wider, within the bound.
A program may use at most 32 MiB of HBM per device.

v0:
```python
import jax
import jax.numpy as jnp
from jax import lax
from jax.sharding import PartitionSpec as P


def silu_parts(gate_pre):
    sigmoid_val = jax.nn.sigmoid(gate_pre)
    return (gate_pre * sigmoid_val, sigmoid_val * (1.0 + gate_pre * (1.0 - sigmoid_val)))


def body(tokens, grad_out, expert_ids, route_weights, w_gate, w_up, w_down):
    wide_count = lax.axis_size("wide")
    narrow_count = lax.axis_size("narrow")
    local_experts = w_gate.shape[0]
    experts_all = local_experts * wide_count
    tok_count = expert_ids.shape[0]
    top_count = expert_ids.shape[1]
    copies = tok_count * top_count
    capacity = min(tok_count, 2 * tok_count * top_count // experts_all)
    slots = experts_all * capacity
    per_column = local_experts * capacity
    feature_cols = tokens.shape[1]
    flat_ids = expert_ids.reshape(copies)
    onehot = (flat_ids[:, None] == jnp.arange(experts_all, dtype=jnp.int32)[None, :]).astype(
        jnp.int32
    )
    before = jnp.cumsum(onehot, axis=0) - onehot
    rank_in = jnp.sum(before * onehot, axis=1)
    target = flat_ids * capacity + rank_in
    place_float = (jnp.arange(slots, dtype=jnp.int32)[:, None] == target[None, :]).astype(
        jnp.float32
    )
    token_place = jnp.sum(place_float.reshape(slots, tok_count, top_count), axis=2).astype(
        jnp.bfloat16
    )
    weight_flat = route_weights.reshape(copies).astype(jnp.float32)
    slot_weight = jnp.sum(place_float * weight_flat[None, :], axis=1).astype(jnp.bfloat16)
    send_tokens = jnp.dot(token_place, tokens, preferred_element_type=jnp.float32).astype(
        jnp.bfloat16
    )
    send_grads = jnp.dot(token_place, grad_out, preferred_element_type=jnp.float32).astype(
        jnp.bfloat16
    )
    got_tokens, got_grads, got_weight = (
        lax.all_to_all(
            send_tokens.reshape(wide_count, per_column, feature_cols),
            "wide",
            split_axis=0,
            concat_axis=0,
            tiled=True,
        ),
        lax.all_to_all(
            send_grads.reshape(wide_count, per_column, feature_cols),
            "wide",
            split_axis=0,
            concat_axis=0,
            tiled=True,
        ),
        lax.all_to_all(
            slot_weight.reshape(wide_count, per_column),
            "wide",
            split_axis=0,
            concat_axis=0,
            tiled=True,
        ),
    )
    full_tokens, full_grads = (
        lax.all_gather(got_tokens, "narrow", axis=2, tiled=True),
        lax.all_gather(got_grads, "narrow", axis=2, tiled=True),
    )
    model_width = full_tokens.shape[2]
    grid_shape = (wide_count, local_experts, capacity, model_width)
    token_rows = full_tokens.reshape(grid_shape)
    grad_rows = full_grads.reshape(grid_shape)
    slot_gain = got_weight.astype(jnp.float32).reshape(wide_count, local_experts, capacity)
    gate_pre = jnp.einsum("sjcd,jdf->sjcf", token_rows, w_gate, preferred_element_type=jnp.float32)
    up_pre = jnp.einsum("sjcd,jdf->sjcf", token_rows, w_up, preferred_element_type=jnp.float32)
    active, gate_slope = silu_parts(gate_pre)
    hidden = (active * up_pre).astype(jnp.bfloat16)
    back_proj = jnp.einsum("sjcd,jfd->sjcf", grad_rows, w_down, preferred_element_type=jnp.float32)
    d_hidden = slot_gain[..., None] * back_proj
    d_gate = (d_hidden * up_pre * gate_slope).astype(jnp.bfloat16)
    d_up = (d_hidden * active).astype(jnp.bfloat16)
    scaled = (slot_gain[..., None] * grad_rows).astype(jnp.bfloat16)
    grad_down = jnp.einsum(
        "sjcf,sjcd->jfd", hidden, scaled, preferred_element_type=jnp.float32
    ).astype(jnp.bfloat16)
    tokens_part = jnp.einsum("sjcf,jdf->sjcd", d_gate, w_gate, preferred_element_type=jnp.float32)
    tokens_part = tokens_part + jnp.einsum(
        "sjcf,jdf->sjcd", d_up, w_up, preferred_element_type=jnp.float32
    )
    tokens_part = tokens_part.reshape(wide_count, per_column, model_width)
    route_part = jnp.sum(hidden.astype(jnp.float32) * back_proj, axis=3).reshape(
        wide_count, per_column
    )
    spread = jnp.broadcast_to(route_part[:, :, None], (wide_count, per_column, narrow_count))
    tokens_share, route_cols = (
        lax.psum_scatter(
            tokens_part.astype(jnp.bfloat16), "narrow", scatter_dimension=2, tiled=True
        ).astype(jnp.float32),
        lax.psum_scatter(
            spread.astype(jnp.bfloat16), "narrow", scatter_dimension=2, tiled=True
        ).astype(jnp.float32),
    )
    route_share = route_cols[:, :, 0]
    back_tokens, back_route = (
        lax.all_to_all(
            tokens_share.astype(jnp.bfloat16), "wide", split_axis=0, concat_axis=0, tiled=True
        ),
        lax.all_to_all(
            route_share.astype(jnp.bfloat16), "wide", split_axis=0, concat_axis=0, tiled=True
        ),
    )
    slot_grads = back_tokens.reshape(slots, feature_cols)
    slot_route = back_route.reshape(slots).astype(jnp.float32)
    grad_tokens = lax.dot_general(
        token_place, slot_grads, (((0,), (0,)), ((), ())), preferred_element_type=jnp.float32
    ).astype(jnp.bfloat16)
    grad_route = (
        jnp.sum(place_float * slot_route[:, None], axis=0)
        .reshape(tok_count, top_count)
        .astype(jnp.bfloat16)
    )
    return (grad_tokens, grad_route, grad_down)


def solution(mesh):
    in_specs = (
        P("wide", "narrow"),
        P("wide", "narrow"),
        P("wide", None),
        P("wide", None),
        P("wide", None, "narrow"),
        P("wide", None, "narrow"),
        P("wide", "narrow", None),
    )
    out_specs = (P("wide", "narrow"), P("wide", None), P("wide", "narrow", None))
    return jax.shard_map(body, mesh=mesh, in_specs=in_specs, out_specs=out_specs, check_vma=False)
```

profile of v0, /device:TPU:1, one launch (start us, length us, event | category | flops | bytes accessed | tf_op | source)
XLA Modules:
  0.0 414.2 jit_solution(14498964032655539800)
XLA Ops:
  7.2 0.0 all-gather.5.cloned.1.call-start
  7.2 0.8 copy.38
  8.0 0.1 eq.43
  8.2 0.6 reduce-window.6
  8.8 0.2 slice_reduce_fusion
  9.0 0.1 bitcast_bitcast_fusion
  9.1 0.1 reduce_sum.48
  9.2 0.2 convert_reduce_fusion
  9.4 0.9 convolution_convert_fusion
  10.4 0.1 reshape.155
  10.5 29.4 %all_to_all.27 = bf16[64,6,256]{2,1,0:T(8,128)(2,1)S(1)} all-to-all(bf16[64,6,256]{2,1,0:T(8,128)(2,1)S(1)} %reshape.155), channel_id=1, replica_groups=mesh['wide'=64,'narrow'=16] {'wide'}, dimensions={0} | all-to-all | bytes 393216 | tf_op jit(solution)/shard_map/all_to_all | solution.py:46
  39.8 0.7 copy.46
  40.6 0.0 all-gather.3.cloned.1.call-start
  40.6 1.0 convolution_convert_fusion.1
  41.6 0.1 reshape.153
  41.7 17.9 %all_to_all.28 = bf16[64,6,256]{2,1,0:T(8,128)(2,1)S(1)} all-to-all(bf16[64,6,256]{2,1,0:T(8,128)(2,1)S(1)} %reshape.153), channel_id=1, replica_groups=mesh['wide'=64,'narrow'=16] {'wide'}, dimensions={0} | all-to-all | bytes 393216 | tf_op jit(solution)/shard_map/all_to_all | solution.py:53
  59.6 0.7 copy.45
  60.3 1.3 dynamic-slice
  61.6 56.3 %all-gather.5.cloned.1.call-done = bf16[64,6,4096]{2,0,1:T(8,128)(2,1)} async-done(((bf16[64,6,256]{2,0,1:T(8,128)(2,1)}), bf16[64,6,4096]{2,0,1:T(8,128)(2,1)}) %all-gather.5.cloned.1.call-update) | async-done | bytes 3145744 | tf_op jit(solution)/shard_map/all_gather | solution.py:69
  117.9 3.0 convolution_bitcast_fusion.1
  120.9 1.0 convolution_bitcast_fusion.2
  121.9 84.2 %all-gather.3.cloned.1.call-done = bf16[64,6,4096]{2,0,1:T(8,128)(2,1)} async-done(((bf16[64,6,256]{2,0,1:T(8,128)(2,1)}), bf16[64,6,4096]{2,0,1:T(8,128)(2,1)}) %all-gather.3.cloned.1.call-update) | async-done | bytes 3145744 | tf_op jit(solution)/shard_map/all_gather | solution.py:70
  206.1 3.0 multiply_reduce_fusion
  209.1 39.2 %all-reduce.1 = bf16[64,6,16]{0,1,2:T(8,128)(2,1)S(1)} all-reduce(bf16[64,6,16]{0,1,2:T(8,128)(2,1)S(1)} %broadcast_in_dim.2), channel_id=3, replica_groups=mesh['wide'=64,'narrow'=16] {'narrow'}, use_global_device_ids=true, to_apply=%region_7.8.clone | all-reduce | flops 6144 | bytes 24576
  248.3 0.6 dynamic-slice_bitcast_fusion
  249.0 0.7 copy.48
  249.7 35.1 %all-to-all-start.4 = ((bf16[64,1,6]{2,1,0:T(2,128)(2,1)}), bf16[64,1,6]{2,1,0:T(2,128)(2,1)S(1)}, u32[]{:S(2)}, u32[]{:S(2)}) async-start(bf16[64,1,6]{2,1,0:T(2,128)(2,1)} %copy.48), calls=%async_computation.5 | async-start | bytes 65536 | tf_op jit(solution)/shard_map/all_to_all | solution.py:111
  284.8 0.0 reduce-scatter.2.cloned.1.call-start
  284.9 0.1 copy.42
  285.0 0.1 reshape.163
  285.0 9.0 %all-to-all-done.4 = bf16[64,1,6]{2,1,0:T(2,128)(2,1)S(1)} async-done(((bf16[64,1,6]{2,1,0:T(2,128)(2,1)}), bf16[64,1,6]{2,1,0:T(2,128)(2,1)S(1)}, u32[]{:S(2)}, u32[]{:S(2)}) %all-to-all-start.4) | async-done | bytes 800 | tf_op jit(solution)/shard_map/all_to_all | solution.py:111
  294.0 0.1 convert_reduce_fusion.1
  294.1 0.1 reshape.165
  294.3 0.2 select_reduce_fusion
  294.5 0.2 convert_element_type.151
  294.6 13.3 %all_to_all.29 = bf16[64,1,6]{2,1,0:T(2,128)(2,1)S(1)} all-to-all(bf16[64,1,6]{2,1,0:T(2,128)(2,1)S(1)} %convert_element_type.151), channel_id=1, replica_groups=mesh['wide'=64,'narrow'=16] {'wide'}, dimensions={0} | all-to-all | bytes 1536 | tf_op jit(solution)/shard_map/all_to_all | solution.py:60
  308.0 0.1 copy.44
  308.1 1.0 fusion.3
  309.1 2.7 add_convert_fusion
  311.9 61.5 %reduce-scatter.2.cloned.1.call-done = bf16[64,6,256]{2,0,1:T(8,128)(2,1)} async-done(((bf16[64,6,4096]{2,0,1:T(8,128)(2,1)}), bf16[64,6,256]{2,0,1:T(8,128)(2,1)}) %reduce-scatter.2.cloned.1.call-update) | async-done | bytes 196624 | tf_op jit(solution)/shard_map/reduce_scatter | solution.py:99
  373.4 1.8 copy.47
  375.1 19.8 %all-to-all-start.3 = ((bf16[64,6,256]{2,1,0:T(8,128)(2,1)}), bf16[64,6,256]{2,1,0:T(8,128)(2,1)S(1)}, u32[]{:S(2)}, u32[]{:S(2)}) async-start(bf16[64,6,256]{2,1,0:T(8,128)(2,1)} %copy.47), calls=%async_computation.4 | async-start | bytes 524288 | tf_op jit(solution)/shard_map/all_to_all | solution.py:108
  394.9 0.1 convert_element_type.143
  395.0 0.7 copy.50
  395.7 3.6 fusion.1
  399.3 7.6 %all-to-all-done.3 = bf16[64,6,256]{2,1,0:T(8,128)(2,1)S(1)} async-done(((bf16[64,6,256]{2,1,0:T(8,128)(2,1)}), bf16[64,6,256]{2,1,0:T(8,128)(2,1)S(1)}, u32[]{:S(2)}, u32[]{:S(2)}) %all-to-all-start.3) | async-done | bytes 196640 | tf_op jit(solution)/shard_map/all_to_all | solution.py:108
  406.9 0.1 reshape.160
  407.0 0.8 convolution_convert_fusion.2
  (22 shorter events, 0.2 us)
Async XLA Ops:
  7.2 110.7 %copy-start = (bf16[1,4096,96]{1,2,0:T(8,128)(2,1)S(1)}, bf16[1,4096,96]{1,2,0:T(8,128)(2,1)}, u32[]{:S(2)}) copy-start(bf16[1,4096,96]{1,2,0:T(8,128)(2,1)} %param.11) | copy-start | bytes 2359300
  7.2 110.7 %all-gather.5.cloned.1.call-start = ((), (), s32[]{:S(2)}) async-start(), calls=%async_computation.7 | async-start | bytes 3342336 | tf_op jit(solution)/shard_map/all_gather | solution.py:69
  40.5 80.3 %copy-start.2 = (bf16[1,4096,96]{1,2,0:T(8,128)(2,1)S(1)}, bf16[1,4096,96]{1,2,0:T(8,128)(2,1)}, u32[]{:S(2)}) copy-start(bf16[1,4096,96]{1,2,0:T(8,128)(2,1)} %param.12) | copy-start | bytes 2359300
  40.6 165.6 %all-gather.3.cloned.1.call-start = ((), (), s32[]{:S(2)}) async-start(), calls=%async_computation.6 | async-start | bytes 3342336 | tf_op jit(solution)/shard_map/all_gather | solution.py:70
  61.6 144.5 %copy-start.4 = (bf16[1,96,4096]{2,1,0:T(8,128)(2,1)S(1)}, bf16[1,96,4096]{2,1,0:T(8,128)(2,1)}, u32[]{:S(2)}) copy-start(bf16[1,96,4096]{2,1,0:T(8,128)(2,1)} %param.13) | copy-start | bytes 2359300
  117.9 3.0 copy-start.1
  121.9 163.0 %copy-start.3 = (bf16[24,8]{0,1:T(8,128)(2,1)S(1)}, bf16[24,8]{0,1:T(8,128)(2,1)}, u32[]{:S(2)}) copy-start(bf16[24,8]{0,1:T(8,128)(2,1)} %param.10) | copy-start | bytes 1156
  249.7 44.3 %all-to-all-start.4 = ((bf16[64,1,6]{2,1,0:T(2,128)(2,1)}), bf16[64,1,6]{2,1,0:T(2,128)(2,1)S(1)}, u32[]{:S(2)}, u32[]{:S(2)}) async-start(bf16[64,1,6]{2,1,0:T(2,128)(2,1)} %copy.48), calls=%async_computation.5 | async-start | bytes 65536 | tf_op jit(solution)/shard_map/all_to_all | solution.py:111
  284.8 88.6 %reduce-scatter.2.cloned.1.call-start = ((), (), s32[]{:S(2)}) async-start(), calls=%async_computation.8 | async-start | bytes 3342336 | tf_op jit(solution)/shard_map/reduce_scatter | solution.py:99
  375.1 31.8 %all-to-all-start.3 = ((bf16[64,6,256]{2,1,0:T(8,128)(2,1)}), bf16[64,6,256]{2,1,0:T(8,128)(2,1)S(1)}, u32[]{:S(2)}, u32[]{:S(2)}) async-start(bf16[64,6,256]{2,1,0:T(8,128)(2,1)} %copy.47), calls=%async_computation.4 | async-start | bytes 524288 | tf_op jit(solution)/shard_map/all_to_all | solution.py:108
Sparse Core Ops, SparseCore 0:
  40.7 77.1 all-gather.4
  120.4 85.6 all-gather.2
  312.0 61.3 reduce-scatter.1
where the time goes:
time: 415 us; the launch traced here: 414 us
  waiting for transfers between devices  219 us (53%)
  blocking collectives  99.8 us (24%)
  starting transfers between devices  55 us (13%)
  matrix products  17.1 us (4%)
  between operations  13.9 us (3%)
  local copies, waits for them, and re-layouts  8.54 us (2%)
    all_gather x1, waiting for transfers between devices, body(): lax.all_gather(got_grads, 'narrow', axis=2, tiled=True)  84.2 us
    reduce_scatter x1, waiting for transfers between devices, body(): lax.psum_scatter(tokens_part.astype(jnp.bfloat16), 'narrow', scatter_dime...  61.5 us
    all_gather x1, waiting for transfers between devices, body(): lax.all_gather(got_tokens, 'narrow', axis=2, tiled=True)  56.3 us
    unnamed x1, blocking collectives  39.2 us
    all_to_all x1, starting transfers between devices, body(): lax.all_to_all(route_share.astype(jnp.bfloat16), 'wide', split_axis=0, co...  35.1 us
    all_to_all x1, blocking collectives, body(): lax.all_to_all(send_tokens.reshape(wide_count, per_column, feature_cols),...  29.4 us
    all_to_all x1, starting transfers between devices, body(): lax.all_to_all(tokens_share.astype(jnp.bfloat16), 'wide', split_axis=0, c...  19.8 us
    all_to_all x1, blocking collectives, body(): lax.all_to_all(send_grads.reshape(wide_count, per_column, feature_cols),...  17.9 us
  transfers between devices with their start and end apart: 5, of which 5 were waited for; matrix products, arithmetic and copies ran while one was open for 3% of the time, Pallas kernels for 0%

commit v1 on v0

v1 whole, which is shorter than its diff:
```python
import functools

import jax
import jax.numpy as jnp
from jax import lax
from jax.experimental import pallas as pl
from jax.experimental.pallas import tpu as pltpu
from jax.sharding import PartitionSpec as P

MESH = pl.DeviceIdType.MESH
F32 = jnp.float32
BF16 = jnp.bfloat16
LANES = 128


def dot_nn(a, b):
    return lax.dot_general(a, b, (((1,), (0,)), ((), ())), preferred_element_type=F32)


def dot_nt(a, b):
    return lax.dot_general(a, b, (((1,), (1,)), ((), ())), preferred_element_type=F32)


def dot_tn(a, b):
    return lax.dot_general(a, b, (((0,), (0,)), ((), ())), preferred_element_type=F32)


def steps_of(value, width, count):
    out = jnp.zeros_like(value)
    for m in range(1, count):
        out = out + (value >= width * m).astype(jnp.int32)
    return out


def kernel(
    cfg,
    ids_ref,
    rw_ref,
    tok_ref,
    grd_ref,
    wg_ref,
    wu_ref,
    wd_ref,
    gtok_out,
    groute_out,
    gdown_out,
    pack,
    ycol,
    place_t,
    emat,
    slot_key,
    sel,
    gtok,
    ggrd,
    gain,
    wgu,
    wdn,
    acc_gu,
    acc_bp,
    dcat,
    hidden,
    rs_send,
    rs_recv,
    zroute,
    zroute_own,
    rsum,
    xroute,
    cgrad,
    xback,
    yback_send,
    yback,
    gdown,
    y_snd,
    y_rcv,
    x_snd,
    x_rcv,
    g_snd,
    g_rcv,
    r_snd,
    r_rcv,
    z_snd,
    z_rcv,
    xb_snd,
    xb_rcv,
    yb_snd,
    yb_rcv,
    w_sem,
    o_sem,
):
    X, Y, C, Z = cfg["X"], cfg["Y"], cfg["C"], cfg["Z"]
    T, TP, F, H, HP, E, TOP, CAP = (
        cfg[k] for k in ("T", "TP", "F", "H", "HP", "E", "TOP", "CAP")
    )
    NP = X * C
    PB = Y * CAP
    SLOTS = NP * PB
    TOKS = Y * TP
    half = Z // 2
    A = F // 2

    w = lax.axis_index("wide")
    z = lax.axis_index("narrow")
    x = w // (Y * C)
    y = (w // C) % Y
    c = w % C
    me = x * C + c

    def y_peer(d):
        yy = (y + d) % Y
        return yy, (x * (Y * C) + yy * C + c, z)

    def x_peer(d):
        p = (me + d) % NP
        return p, ((p // C) * (Y * C) + y * C + p % C, z)

    right = (w, (z + 1) % Z)
    left = (w, (z + Z - 1) % Z)

    def rows(block, size):
        return pl.ds(pl.multiple_of(block * size, 16), size)

    def cols(block):
        return pl.ds(pl.multiple_of(block * F, LANES), F)

    def remote(src, dst, snd, rcv, device):
        return pltpu.make_async_remote_copy(
            src_ref=src, dst_ref=dst, send_sem=snd, recv_sem=rcv, device_id=device, device_id_type=MESH
        )

    def each(first, last, body):
        lax.fori_loop(first, last, lambda i, carry: (body(i), carry)[1], 0)

    weights = [
        pltpu.make_async_copy(wg_ref, wgu.at[pl.ds(0, H), :], w_sem.at[0]),
        pltpu.make_async_copy(wu_ref, wgu.at[pl.ds(HP, H), :], w_sem.at[1]),
        pltpu.make_async_copy(wd_ref, wdn.at[pl.ds(0, H), :], w_sem.at[2]),
    ]
    for copy in weights:
        copy.start()

    barrier = pltpu.get_barrier_semaphore()

    def greet(device):
        pl.semaphore_signal(barrier, inc=1, device_id=device, device_id_type=MESH)

    each(1, Y, lambda d: greet(y_peer(d)[1]))
    each(1, NP, lambda d: greet(x_peer(d)[1]))
    each(1, Z, lambda d: greet((w, (z + d) % Z)))

    lane = lax.broadcasted_iota(jnp.int32, (TP, LANES), 1)
    lane_expert = jnp.where(lane >= E, lane - E, lane)
    named = jnp.zeros((TP, LANES), F32)
    weight = jnp.zeros((TP, LANES), F32)
    for k in range(TOP):
        hit = ids_ref[:, k : k + 1] == lane_expert
        named = named + jnp.where(hit, 1.0, 0.0)
        weight = weight + jnp.where(hit, rw_ref[:, k : k + 1], 0.0)
    tri = (
        lax.broadcasted_iota(jnp.int32, (TP, TP), 0) > lax.broadcasted_iota(jnp.int32, (TP, TP), 1)
    ).astype(F32)
    before = dot_nn(tri.astype(BF16), named.astype(BF16))
    table = jnp.where(lane < E, named * (before + 1.0), jnp.where(lane < 2 * E, weight, 0.0))

    pack[...] = jnp.zeros_like(pack)
    pack[0:T, 0:F] = tok_ref[...]
    pack[:, F : F + LANES] = table.astype(BF16)
    pack[0:T, F + LANES :] = grd_ref[...]

    pl.semaphore_wait(barrier, (Y - 1) + (NP - 1) + (Z - 1))

    parts = (pl.ds(0, F + LANES), pl.ds(F + LANES, F))

    def y_copy(part, d, owner, device):
        return remote(
            pack.at[:, parts[part]],
            ycol.at[rows(owner, TP), parts[part]],
            y_snd.at[part, d],
            y_rcv.at[part, d],
            device,
        )

    for part in range(2):
        each(1, Y, lambda d, part=part: y_copy(part, d, y, y_peer(d)[1]).start())
    ycol[rows(y, TP), :] = pack[...]

    slot = lax.broadcasted_iota(jnp.int32, (SLOTS, LANES), 0)
    slot_lane = lax.broadcasted_iota(jnp.int32, (SLOTS, LANES), 1)
    peer = steps_of(slot, PB, NP)
    peer_x = steps_of(peer, C, X)
    expert = peer_x * (Y * C) + y * C + (peer - peer_x * C)
    emat[0] = (slot_lane == expert).astype(F32).astype(BF16)
    emat[1] = (slot_lane == expert + E).astype(F32).astype(BF16)
    slot = lax.broadcasted_iota(jnp.int32, (SLOTS, TOKS), 0)
    tok_y = steps_of(lax.broadcasted_iota(jnp.int32, (SLOTS, TOKS), 1), TP, Y)
    inner = slot - PB * steps_of(slot, PB, NP)
    slot_y = steps_of(inner, CAP, Y)
    slot_key[...] = jnp.where(tok_y == slot_y, inner - CAP * slot_y + 1, -1).astype(F32)

    wgu[H:HP, :] = jnp.zeros((HP - H, wgu.shape[1]), BF16)
    wgu[HP + H :, :] = jnp.zeros((HP - H, wgu.shape[1]), BF16)
    wdn[H:, :] = jnp.zeros((HP - H, wdn.shape[1]), BF16)

    def y_wait(part):
        each(1, Y, lambda d: y_copy(part, d, (y + Y - d) % Y, y_peer(d)[1]).wait_recv())

    y_wait(0)
    tables = ycol[:, F : F + LANES]
    place = dot_nt(emat[0], tables) == slot_key[...]
    place_b = place.astype(F32).astype(BF16)
    sel[:, 0:F] = dot_nn(place_b, ycol[:, 0:F]).astype(BF16)

    def x_copy(part, d, src, dst, device):
        if part == 0:
            return remote(
                sel.at[rows(src, PB), pl.ds(0, F)],
                gtok.at[z, rows(dst, PB), :],
                x_snd.at[0, d],
                x_rcv.at[0, d],
                device,
            )
        if part == 1:
            return remote(
                sel.at[rows(src, PB), pl.ds(F, F)],
                ggrd.at[z, rows(dst, PB), :],
                x_snd.at[1, d],
                x_rcv.at[1, d],
                device,
            )
        return remote(
            sel.at[rows(src, PB), pl.ds(2 * F, LANES)],
            gain.at[rows(dst, PB), :],
            x_snd.at[2, d],
            x_rcv.at[2, d],
            device,
        )

    def x_start(part):
        def one(d):
            p, device = x_peer(d)
            x_copy(part, d, p, me, device).start()

        each(1, NP, one)

    def x_wait(part):
        def one(d):
            p = (me + NP - d) % NP
            x_copy(part, d, p, p, x_peer(d)[1]).wait_recv()

        each(1, NP, one)

    x_start(0)
    gtok[z, rows(me, PB), :] = sel[rows(me, PB), 0:F]

    y_wait(1)
    sel[:, F : 2 * F] = dot_nn(place_b, ycol[:, F + LANES :]).astype(BF16)
    x_start(1)
    weights_of = jnp.where(place, dot_nt(emat[1], tables), 0.0)
    sel[:, 2 * F :] = jnp.broadcast_to(
        jnp.sum(weights_of, axis=1, keepdims=True), (SLOTS, LANES)
    ).astype(BF16)
    x_start(2)
    ggrd[z, rows(me, PB), :] = sel[rows(me, PB), F : 2 * F]
    gain[rows(me, PB), :] = sel[rows(me, PB), 2 * F :]

    def hop(stream, s, sending):
        to_right = stream % 2 == 0
        buf = gtok if stream < 2 else ggrd
        back = s if sending else s + 1
        owner = (z + Z - back) % Z if to_right else (z + back) % Z
        return remote(
            buf.at[owner],
            buf.at[owner],
            g_snd.at[stream, s],
            g_rcv.at[stream, s],
            right if to_right else left,
        )

    def use_tokens(owner):
        acc_gu[...] += dot_nt(gtok[owner], wgu[:, cols(owner)])

    def use_grads(owner):
        acc_bp[...] += dot_nt(ggrd[owner], wdn[:, cols(owner)])

    x_wait(0)
    hop(0, 0, True).start()
    hop(1, 0, True).start()
    acc_gu[...] = jnp.zeros_like(acc_gu)
    acc_bp[...] = jnp.zeros_like(acc_bp)
    x_wait(1)
    hop(2, 0, True).start()
    hop(3, 0, True).start()
    for copy in weights:
        copy.wait()
    use_tokens(z)
    use_grads(z)

    key_slot = lax.broadcasted_iota(jnp.int32, (TOKS, SLOTS), 1)
    key_inner = key_slot - PB * steps_of(key_slot, PB, NP)
    key_y = steps_of(key_inner, CAP, Y)
    key_tok = steps_of(lax.broadcasted_iota(jnp.int32, (TOKS, SLOTS), 0), TP, Y)
    key = jnp.where(key_tok == key_y, key_inner - CAP * key_y + 1, -1).astype(F32)
    place_t[...] = (dot_nt(ycol[:, F : F + LANES], emat[0]) == key).astype(F32).astype(BF16)
    x_wait(2)

    def gather_step(s):
        hop(0, s - 1, False).wait_recv()
        hop(0, s, True).start()
        hop(1, s - 1, False).wait_recv()

        @pl.when(s < half - 1)
        def _():
            hop(1, s, True).start()

        hop(2, s - 1, False).wait_recv()

        @pl.when(s < half - 1)
        def _():
            hop(2, s, True).start()

        hop(3, s - 1, False).wait_recv()
        hop(3, s, True).start()
        use_tokens((z + Z - s) % Z)
        use_tokens((z + s) % Z)
        use_grads((z + Z - s) % Z)
        use_grads((z + s) % Z)

    each(1, half, gather_step)
    hop(0, half - 1, False).wait_recv()
    use_tokens((z + half) % Z)
    hop(3, half - 1, False).wait_recv()
    use_grads((z + half) % Z)

    gate = acc_gu[:, 0:HP]
    up = acc_gu[:, HP:]
    back = acc_bp[...]
    scale = gain[...].astype(F32)
    sig = jax.nn.sigmoid(gate)
    active = gate * sig
    slope = sig * (1.0 + gate * (1.0 - sig))
    hid = (active * up).astype(BF16)
    hidden[...] = hid
    d_hidden = scale * back
    dcat[:, 0:HP] = (d_hidden * up * slope).astype(BF16)
    dcat[:, HP:] = (d_hidden * active).astype(BF16)
    route = jnp.sum(hid.astype(F32) * back, axis=1, keepdims=True)

    def ring(stream, k):
        return remote(
            rs_send.at[stream, k],
            rs_recv.at[stream, k],
            r_snd.at[stream, k],
            r_rcv.at[stream, k],
            right if stream < 2 else left,
        )

    def partial(owner):
        return dot_nn(dcat[...], wgu[:, cols(owner)])

    def push(stream, k, value, add):
        if add:
            ring(stream, k + 1).wait_recv()
            value = value + rs_recv[stream, k + 1].astype(F32)
        rs_send[stream, k] = value.astype(BF16)
        ring(stream, k).start()

    def down(chunk):
        scaled = (jnp.concatenate([scale_ref()] * (F // LANES), axis=1) * ggrd[chunk].astype(F32)).astype(BF16)
        gdown[:, cols(chunk)] = dot_tn(hidden[...], scaled)[0:H, :].astype(BF16)

    def scale_ref():
        return gain[...].astype(F32)

    far = partial((z + half) % Z)
    push(0, half, far[:, 0:A], False)
    push(3, half, far[:, A:], False)
    to_right = partial((z + half - 1) % Z)
    to_left = partial((z + Z - half + 1) % Z)
    push(1, half - 1, to_right[:, A:], False)
    push(2, half - 1, to_left[:, 0:A], False)

    rt_row = lax.broadcasted_iota(jnp.int32, (SLOTS, LANES), 0)
    rt_inner = rt_row - PB * steps_of(rt_row, PB, NP)
    rt_lane = lax.broadcasted_iota(jnp.int32, (SLOTS, LANES), 1)
    spread = jnp.where(rt_lane == rt_inner, route.astype(BF16).astype(F32), 0.0).astype(BF16)
    blk = lax.broadcasted_iota(jnp.int32, (8, SLOTS), 0)
    blk_of = steps_of(lax.broadcasted_iota(jnp.int32, (8, SLOTS), 1), PB, NP)
    pick = (blk == blk_of).astype(F32).astype(BF16)
    zroute_own[...] = dot_nn(pick, spread)

    def z_copy(d, slot_d, device):
        return remote(zroute_own, zroute.at[slot_d], z_snd.at[d], z_rcv.at[d], device)

    each(1, Z, lambda d: z_copy(d, d, (w, (z + d) % Z)).start())

    push(0, half - 1, to_right[:, 0:A], True)
    push(3, half - 1, to_left[:, A:], True)
    for chunk in range(2):
        down(chunk)

    def reduce_step(i):
        k = half - 1 - i
        to_right = partial((z + k) % Z)
        to_left = partial((z + Z - k) % Z)
        push(0, k, to_right[:, 0:A], True)
        push(3, k, to_left[:, A:], True)
        push(1, k, to_right[:, A:], True)
        push(2, k, to_left[:, 0:A], True)
        per = -(-(Z - 2) // (half - 2))
        for j in range(per):
            chunk = 2 + (i - 1) * per + j

            @pl.when(chunk < Z)
            def _():
                down(chunk)

    each(1, half - 1, reduce_step)
    out_copy = pltpu.make_async_copy(gdown, gdown_out, o_sem)
    out_copy.start()

    each(1, Z, lambda d: z_copy(d, d, (w, (z + d) % Z)).wait_recv())
    total = zroute_own[...]
    for d in range(1, Z):
        total = total + zroute[d]
    rsum[...] = total.astype(BF16).astype(F32)

    def xb_copy(part, d, src, dst, device):
        if part == 0:
            return remote(rsum, xroute.at[dst], xb_snd.at[0, d], xb_rcv.at[0, d], device)
        return remote(
            cgrad.at[rows(src, PB), :],
            xback.at[rows(dst, PB), :],
            xb_snd.at[1, d],
            xb_rcv.at[1, d],
            device,
        )

    def xb_start(part):
        def one(d):
            p, device = x_peer(d)
            xb_copy(part, d, p, me, device).start()

        each(1, NP, one)

    def xb_wait(part):
        def one(d):
            p = (me + NP - d) % NP
            xb_copy(part, d, p, p, x_peer(d)[1]).wait_recv()

        each(1, NP, one)

    xb_start(0)
    xroute[me] = rsum[...]

    own = partial(z)
    for lanes, streams in ((slice(0, A), (0, 2)), (slice(A, F), (1, 3))):
        value = own[:, lanes]
        for stream in streams:
            ring(stream, 1).wait_recv()
            value = value + rs_recv[stream, 1].astype(F32)
        cgrad[:, lanes] = value.astype(BF16)
    xb_start(1)
    xback[rows(me, PB), :] = cgrad[rows(me, PB), :]

    xb_wait(0)
    sub = lax.broadcasted_iota(jnp.int32, (NP, 8, LANES), 1)
    mine = jnp.sum(jnp.where(sub == me, xroute[...], 0.0), axis=1).astype(BF16)
    lane_in = lax.broadcasted_iota(jnp.int32, (LANES, SLOTS), 0)
    slot_in = lax.broadcasted_iota(jnp.int32, (LANES, SLOTS), 1)
    slot_in = slot_in - PB * steps_of(slot_in, PB, NP)
    wide_rows = dot_nn(mine, (lane_in == slot_in).astype(F32).astype(BF16))
    from_peer = lax.broadcasted_iota(jnp.int32, (NP, SLOTS), 0)
    slot_peer = steps_of(lax.broadcasted_iota(jnp.int32, (NP, SLOTS), 1), PB, NP)
    values = jnp.sum(jnp.where(from_peer == slot_peer, wide_rows, 0.0), axis=0, keepdims=True)
    routed = (place_t[...].astype(F32) * values).astype(BF16)
    yback_send[:, F:] = dot_nn(routed, emat[0]).astype(BF16)

    xb_wait(1)
    yback_send[:, 0:F] = dot_nn(place_t[...], xback[...]).astype(BF16)

    def yb_copy(d, src, dst, device):
        return remote(
            yback_send.at[rows(src, TP), :], yback.at[rows(dst, TP), :], yb_snd.at[d], yb_rcv.at[d], device
        )

    def yb_start(d):
        yy, device = y_peer(d)
        yb_copy(d, yy, y, device).start()

    each(1, Y, yb_start)
    yback[rows(y, TP), :] = yback_send[rows(y, TP), :]

    def yb_wait(d):
        yy = (y + Y - d) % Y
        yb_copy(d, yy, yy, y_peer(d)[1]).wait_recv()

    each(1, Y, yb_wait)
    final = jnp.zeros((TP, F + LANES), F32)
    for j in range(Y):
        final = final + yback[j * TP : (j + 1) * TP, :].astype(F32)
    gtok_out[...] = final[0:T, 0:F].astype(BF16)
    per_expert = final[:, F:]
    out_lane = lax.broadcasted_iota(jnp.int32, (TP, TOP), 1)
    result = jnp.zeros((TP, TOP), F32)
    for k in range(TOP):
        hit = (ids_ref[:, k : k + 1] == lane_expert) & (lane < E)
        value = jnp.sum(jnp.where(hit, per_expert, 0.0), axis=1, keepdims=True)
        result = result + jnp.where(out_lane == k, value, 0.0)
    groute_out[...] = result[0:T, :].astype(BF16)

    for part in range(2):
        each(1, Y, lambda d, part=part: y_copy(part, d, y, y_peer(d)[1]).wait_send())
    for part in range(3):
        each(1, NP, lambda d, part=part: x_copy(part, d, x_peer(d)[0], me, x_peer(d)[1]).wait_send())
    for stream in range(4):
        n = half if stream in (0, 3) else half - 1
        each(0, n, lambda s, stream=stream: hop(stream, s, True).wait_send())
        each(1, n + 1, lambda k, stream=stream: ring(stream, k).wait_send())
    each(1, Z, lambda d: z_copy(d, d, (w, (z + d) % Z)).wait_send())
    for part in range(2):
        each(1, NP, lambda d, part=part: xb_copy(part, d, x_peer(d)[0], me, x_peer(d)[1]).wait_send())
    each(1, Y, lambda d: yb_copy(d, y_peer(d)[0], y, y_peer(d)[1]).wait_send())
    out_copy.wait()


GRID = {64: (4, 8, 2), 8: (2, 2, 2)}


def body(tokens, grad_out, expert_ids, route_weights, w_gate, w_up, w_down):
    X, Y, C = GRID[lax.axis_size("wide")]
    Z = lax.axis_size("narrow")
    T, F = tokens.shape
    TOP = expert_ids.shape[1]
    D, H = w_gate.shape[1:]
    E = X * Y * C
    CAP = min(T, 2 * T * TOP // E)
    TP = -(-T // 16) * 16
    HP = -(-H // LANES) * LANES
    NP = X * C
    PB = Y * CAP
    SLOTS = NP * PB
    TOKS = Y * TP
    half = Z // 2
    A = F // 2
    cfg = dict(X=X, Y=Y, C=C, Z=Z, T=T, TP=TP, F=F, H=H, HP=HP, E=E, TOP=TOP, CAP=CAP)
    ids = jnp.pad(expert_ids, ((0, TP - T), (0, 0)), constant_values=-1)
    gains = jnp.pad(route_weights.astype(F32), ((0, TP - T), (0, 0)))
    vmem = pl.BlockSpec(memory_space=pltpu.VMEM)
    hbm = pl.BlockSpec(memory_space=pl.ANY)
    dma = pltpu.SemaphoreType.DMA
    scratch = [
        pltpu.VMEM((TP, 2 * F + LANES), BF16),
        pltpu.VMEM((TOKS, 2 * F + LANES), BF16),
        pltpu.VMEM((TOKS, SLOTS), BF16),
        pltpu.VMEM((2, SLOTS, LANES), BF16),
        pltpu.VMEM((SLOTS, TOKS), F32),
        pltpu.VMEM((SLOTS, 2 * F + LANES), BF16),
        pltpu.VMEM((Z, SLOTS, F), BF16),
        pltpu.VMEM((Z, SLOTS, F), BF16),
        pltpu.VMEM((SLOTS, LANES), BF16),
        pltpu.VMEM((2 * HP, D), BF16),
        pltpu.VMEM((HP, D), BF16),
        pltpu.VMEM((SLOTS, 2 * HP), F32),
        pltpu.VMEM((SLOTS, HP), F32),
        pltpu.VMEM((SLOTS, 2 * HP), BF16),
        pltpu.VMEM((SLOTS, HP), BF16),
        pltpu.VMEM((4, half + 1, SLOTS, A), BF16),
        pltpu.VMEM((4, half + 1, SLOTS, A), BF16),
        pltpu.VMEM((Z, 8, LANES), F32),
        pltpu.VMEM((8, LANES), F32),
        pltpu.VMEM((8, LANES), F32),
        pltpu.VMEM((NP, 8, LANES), F32),
        pltpu.VMEM((SLOTS, F), BF16),
        pltpu.VMEM((SLOTS, F), BF16),
        pltpu.VMEM((TOKS, F + LANES), BF16),
        pltpu.VMEM((TOKS, F + LANES), BF16),
        pltpu.VMEM((H, D), BF16),
        dma((2, Y)),
        dma((2, Y)),
        dma((3, NP)),
        dma((3, NP)),
        dma((4, half)),
        dma((4, half)),
        dma((4, half + 1)),
        dma((4, half + 1)),
        dma((Z,)),
        dma((Z,)),
        dma((2, NP)),
        dma((2, NP)),
        dma((Y,)),
        dma((Y,)),
        dma((3,)),
        dma,
    ]
    grad_tokens, grad_route, grad_down = pl.pallas_call(
        functools.partial(kernel, cfg),
        out_shape=(
            jax.ShapeDtypeStruct((T, F), BF16),
            jax.ShapeDtypeStruct((T, TOP), BF16),
            jax.ShapeDtypeStruct((H, D), BF16),
        ),
        in_specs=[vmem] * 4 + [hbm] * 3,
        out_specs=(vmem, vmem, hbm),
        scratch_shapes=scratch,
        compiler_params=pltpu.CompilerParams(
            collective_id=0, has_side_effects=True, vmem_limit_bytes=60 * 1024 * 1024
        ),
        name="experts",
    )(ids, gains, tokens, grad_out, w_gate[0].T, w_up[0].T, w_down[0])
    return grad_tokens, grad_route, grad_down[None]


def solution(mesh):
    in_specs = (
        P("wide", "narrow"),
        P("wide", "narrow"),
        P("wide", None),
        P("wide", None),
        P("wide", None, "narrow"),
        P("wide", None, "narrow"),
        P("wide", "narrow", None),
    )
    out_specs = (P("wide", "narrow"), P("wide", None), P("wide", "narrow", None))
    return jax.shard_map(body, mesh=mesh, in_specs=in_specs, out_specs=out_specs, check_vma=False)
```

time: 415 us -> 169 us (0.41)
  waiting for transfers between devices: 219 us -> 0 us
  Pallas kernels: 0 us -> 162 us
  blocking collectives: 99.8 us -> 0 us
  starting transfers between devices: 55 us -> 0 us
  matrix products: 17.1 us -> 0 us
  between operations: 13.9 us -> 0.66 us
    pallas_call x0 -> x1, Pallas kernels: none -> 162 us  [body(): pl.pallas_call(functools.partial(kernel, cfg), out_shape=(jax.ShapeDtypeS...]
    all_gather x2 -> x0, waiting for transfers between devices: 140 us -> none  [the longest x1 84.2 us: body(): lax.all_gather(got_grads, 'narrow', axis=2, tiled=True)]
    reduce_scatter x1 -> x0, waiting for transfers between devices: 61.5 us -> none  [body(): lax.psum_scatter(tokens_part.astype(jnp.bfloat16), 'narrow', scatter_dime...]
    all_to_all x3 -> x0, blocking collectives: 60.6 us -> none  [the longest x1 29.4 us: body(): lax.all_to_all(send_tokens.reshape(wide_count, per_column, feature_cols),...]
    all_to_all x2 -> x0, starting transfers between devices: 54.9 us -> none  [the longest x1 35.1 us: body(): lax.all_to_all(route_share.astype(jnp.bfloat16), 'wide', split_axis=0, co...]
    unnamed x1 -> x0, blocking collectives: 39.2 us -> none
    dot_general x9 -> x0, matrix products: 17.1 us -> none  [the longest x1 3.63 us: body(): jnp.einsum('sjcf,sjcd->jfd', hidden, scaled, preferred_element_type=jnp.f...]
    all_to_all x2 -> x0, waiting for transfers between devices: 16.6 us -> none  [the longest x1 9 us: body(): lax.all_to_all(route_share.astype(jnp.bfloat16), 'wide', split_axis=0, co...]
  transfers between devices with their start and end apart: 5 -> 0, of which waited for: 5 -> 0; matrix products, arithmetic and copies ran while one was open for 3% -> 0% of each run, Pallas kernels for 0% -> 0%
where the time goes in v1:
time: 169 us; the launch traced here: 168 us
  Pallas kernels  162 us (96%)
  local copies, waits for them, and re-layouts  5.54 us (3%)
    pallas_call x1, Pallas kernels, body(): pl.pallas_call(functools.partial(kernel, cfg), out_shape=(jax.ShapeDtypeS...  162 us
    unnamed x11, local copies, waits for them, and re-layouts  4.93 us

profile of v1, /device:TPU:1, one launch (start us, length us, event | category | flops | bytes accessed | tf_op | source)
XLA Modules:
  0.0 168.4 jit_solution(16915131092535471374)
XLA Ops:
  0.6 0.0 copy-start.2
  0.6 0.7 copy-done.2
  1.3 0.1 copy.11
  1.4 0.0 copy-start.1
  1.4 0.6 pad_convert_fusion.rw_ref
  2.0 0.1 copy-done.1
  2.1 0.1 copy.10
  2.2 0.6 pad.10.ids_ref
  2.8 161.6 %experts.1 = (bf16[24,256]{1,0:T(8,128)(2,1)}, bf16[24,8]{1,0:T(8,128)(2,1)}, bf16[96,4096]{1,0:T(8,128)(2,1)}) custom-call(s32[32,8]{1,0:T(8,128)} %pad.10.ids_ref, f32[32,8]{1,0:T(8,128)} %pad_convert_fusion.rw_ref, bf16[24,256]{1,0:T(8,128)(2,1)} %tok_ref.1, bf16[24,256]{1,0:T(8,128)(2,1)} %grd_ref.1, bf16[96,4096]{1,0:T(8,128)(2,1)} %bitcast.9, ...), custom_call_target="tpu_custom_call" | custom-call | tf_op jit(solution)/shard_map/experts/pallas_call | solution.py:594
  164.4 0.0 copy-start
  164.4 1.3 copy.12
  165.7 0.0 copy-done
  165.7 0.6 copy.15
  166.3 2.1 %copy.16 = bf16[1,96,4096]{2,1,0:T(8,128)(2,1)} copy(bf16[1,96,4096]{2,1,0:T(8,128)(2,1)} %bitcast.8) | data formatting | bytes 1572864
Async XLA Ops:
  0.6 0.7 copy-start.2
  1.4 0.7 copy-start.1
  164.4 1.4 copy-start

commit v2 on v1

--- a/solution.py
+++ b/solution.py
@@ -46,11 +46,15 @@
     gdown_out,
     pack,
     ycol,
+    place_s,
     place_t,
     emat,
     slot_key,
     sel,
     gtok,
+    graw,
+    gycol,
+    gsel,
     ggrd,
     gain,
     wgu,
@@ -74,6 +78,12 @@
     y_rcv,
     x_snd,
     x_rcv,
+    zg_snd,
+    zg_rcv,
+    yg_snd,
+    yg_rcv,
+    xg_snd,
+    xg_rcv,
     g_snd,
     g_rcv,
     r_snd,
@@ -163,25 +173,90 @@
 
     pack[...] = jnp.zeros_like(pack)
     pack[0:T, 0:F] = tok_ref[...]
-    pack[:, F : F + LANES] = table.astype(BF16)
-    pack[0:T, F + LANES :] = grd_ref[...]
+    pack[:, F:] = table.astype(BF16)
+    graw[z, 0:T, :] = grd_ref[...]
+    graw[:, T:, :] = jnp.zeros((Z, TP - T, F), BF16)
 
     pl.semaphore_wait(barrier, (Y - 1) + (NP - 1) + (Z - 1))
 
-    parts = (pl.ds(0, F + LANES), pl.ds(F + LANES, F))
-
-    def y_copy(part, d, owner, device):
+    def y_copy(d, owner, device):
+        return remote(pack, ycol.at[rows(owner, TP), :], y_snd.at[d], y_rcv.at[d], device)
+
+    each(1, Y, lambda d: y_copy(d, y, y_peer(d)[1]).start())
+
+    def zg_copy(d, owner, device):
+        here = graw.at[owner, pl.ds(0, T), :]
+        return remote(here, here, zg_snd.at[d], zg_rcv.at[d], device)
+
+    def yg_copy(chunk, d, owner, device):
         return remote(
-            pack.at[:, parts[part]],
-            ycol.at[rows(owner, TP), parts[part]],
-            y_snd.at[part, d],
-            y_rcv.at[part, d],
+            graw.at[chunk, pl.ds(0, T), :],
+            gycol.at[chunk, pl.ds(pl.multiple_of(owner * TP, 16), T), :],
+            yg_snd.at[chunk, d],
+            yg_rcv.at[chunk, d],
             device,
         )
 
-    for part in range(2):
-        each(1, Y, lambda d, part=part: y_copy(part, d, y, y_peer(d)[1]).start())
+    def xg_copy(chunk, d, src, dst, device):
+        return remote(
+            gsel.at[chunk, rows(src, PB), :],
+            ggrd.at[chunk, rows(dst, PB), :],
+            xg_snd.at[chunk, d],
+            xg_rcv.at[chunk, d],
+            device,
+        )
+
+    each(1, Z, lambda d: zg_copy(d, z, (w, (z + d) % Z)).start())
+
+    def spread_y(chunk):
+        each(1, Y, lambda d: yg_copy(chunk, d, y, y_peer(d)[1]).start())
+        gycol[chunk, rows(y, TP), :] = graw[chunk]
+
+    def arrive_z(chunk):
+        d = (z + Z - chunk) % Z
+        zg_copy(d, chunk, (w, (z + d) % Z)).wait_recv()
+
+    def pair(s, act):
+        act((z + s) % Z)
+
+        @pl.when(s < half)
+        def _():
+            act((z + Z - s) % Z)
+
+    def stage_a(s):
+        def act(chunk):
+            arrive_z(chunk)
+            spread_y(chunk)
+
+        pair(s, act)
+
+    def select(chunk):
+        def one(d):
+            yy = (y + Y - d) % Y
+            yg_copy(chunk, d, yy, y_peer(d)[1]).wait_recv()
+
+        each(1, Y, one)
+        gsel[chunk] = dot_nn(place_s[...], gycol[chunk]).astype(BF16)
+
+        def send(d):
+            p, device = x_peer(d)
+            xg_copy(chunk, d, p, me, device).start()
+
+        each(1, NP, send)
+        ggrd[chunk, rows(me, PB), :] = gsel[chunk, rows(me, PB), :]
+
+    def arrive_x(chunk):
+        def one(d):
+            p = (me + NP - d) % NP
+            xg_copy(chunk, d, p, p, x_peer(d)[1]).wait_recv()
+
+        each(1, NP, one)
+        acc_bp[...] += dot_nt(ggrd[chunk], wdn[:, cols(chunk)])
+
+    spread_y(z)
     ycol[rows(y, TP), :] = pack[...]
+    for j in range(Y):
+        gycol[:, j * TP + T : (j + 1) * TP, :] = jnp.zeros((Z, TP - T, F), BF16)
 
     slot = lax.broadcasted_iota(jnp.int32, (SLOTS, LANES), 0)
     slot_lane = lax.broadcasted_iota(jnp.int32, (SLOTS, LANES), 1)
@@ -200,11 +275,8 @@
     wgu[HP + H :, :] = jnp.zeros((HP - H, wgu.shape[1]), BF16)
     wdn[H:, :] = jnp.zeros((HP - H, wdn.shape[1]), BF16)
 
-    def y_wait(part):
-        each(1, Y, lambda d: y_copy(part, d, (y + Y - d) % Y, y_peer(d)[1]).wait_recv())
-
-    y_wait(0)
-    tables = ycol[:, F : F + LANES]
+    each(1, Y, lambda d: y_copy(d, (y + Y - d) % Y, y_peer(d)[1]).wait_recv())
+    tables = ycol[:, F:]
     place = dot_nt(emat[0], tables) == slot_key[...]
     place_b = place.astype(F32).astype(BF16)
     sel[:, 0:F] = dot_nn(place_b, ycol[:, 0:F]).astype(BF16)
@@ -218,19 +290,11 @@
                 x_rcv.at[0, d],
                 device,
             )
-        if part == 1:
-            return remote(
-                sel.at[rows(src, PB), pl.ds(F, F)],
-                ggrd.at[z, rows(dst, PB), :],
-                x_snd.at[1, d],
-                x_rcv.at[1, d],
-                device,
-            )
         return remote(
-            sel.at[rows(src, PB), pl.ds(2 * F, LANES)],
+            sel.at[rows(src, PB), pl.ds(F, LANES)],
             gain.at[rows(dst, PB), :],
-            x_snd.at[2, d],
-            x_rcv.at[2, d],
+            x_snd.at[1, d],
+            x_rcv.at[1, d],
             device,
         )
 
@@ -250,85 +314,82 @@
 
     x_start(0)
     gtok[z, rows(me, PB), :] = sel[rows(me, PB), 0:F]
-
-    y_wait(1)
-    sel[:, F : 2 * F] = dot_nn(place_b, ycol[:, F + LANES :]).astype(BF16)
-    x_start(1)
+    place_s[...] = place_b
     weights_of = jnp.where(place, dot_nt(emat[1], tables), 0.0)
-    sel[:, 2 * F :] = jnp.broadcast_to(
+    sel[:, F:] = jnp.broadcast_to(
         jnp.sum(weights_of, axis=1, keepdims=True), (SLOTS, LANES)
     ).astype(BF16)
-    x_start(2)
-    ggrd[z, rows(me, PB), :] = sel[rows(me, PB), F : 2 * F]
-    gain[rows(me, PB), :] = sel[rows(me, PB), 2 * F :]
+    x_start(1)
+    gain[rows(me, PB), :] = sel[rows(me, PB), F:]
+    acc_gu[...] = jnp.zeros_like(acc_gu)
+    acc_bp[...] = jnp.zeros_like(acc_bp)
+    stage_a(1)
 
     def hop(stream, s, sending):
         to_right = stream % 2 == 0
-        buf = gtok if stream < 2 else ggrd
         back = s if sending else s + 1
         owner = (z + Z - back) % Z if to_right else (z + back) % Z
-        return remote(
-            buf.at[owner],
-            buf.at[owner],
-            g_snd.at[stream, s],
-            g_rcv.at[stream, s],
-            right if to_right else left,
-        )
+        block = gtok.at[owner, pl.ds((stream // 2) * (SLOTS // 2), SLOTS // 2), :]
+        return remote(block, block, g_snd.at[stream, s], g_rcv.at[stream, s], right if to_right else left)
 
     def use_tokens(owner):
         acc_gu[...] += dot_nt(gtok[owner], wgu[:, cols(owner)])
 
-    def use_grads(owner):
-        acc_bp[...] += dot_nt(ggrd[owner], wdn[:, cols(owner)])
-
     x_wait(0)
-    hop(0, 0, True).start()
-    hop(1, 0, True).start()
-    acc_gu[...] = jnp.zeros_like(acc_gu)
-    acc_bp[...] = jnp.zeros_like(acc_bp)
-    x_wait(1)
-    hop(2, 0, True).start()
-    hop(3, 0, True).start()
+    for stream in range(4):
+        hop(stream, 0, True).start()
+    select(z)
+    stage_a(2)
     for copy in weights:
         copy.wait()
     use_tokens(z)
-    use_grads(z)
 
     key_slot = lax.broadcasted_iota(jnp.int32, (TOKS, SLOTS), 1)
     key_inner = key_slot - PB * steps_of(key_slot, PB, NP)
     key_y = steps_of(key_inner, CAP, Y)
     key_tok = steps_of(lax.broadcasted_iota(jnp.int32, (TOKS, SLOTS), 0), TP, Y)
     key = jnp.where(key_tok == key_y, key_inner - CAP * key_y + 1, -1).astype(F32)
-    place_t[...] = (dot_nt(ycol[:, F : F + LANES], emat[0]) == key).astype(F32).astype(BF16)
-    x_wait(2)
+    place_t[...] = (dot_nt(ycol[:, F:], emat[0]) == key).astype(F32).astype(BF16)
+    x_wait(1)
+
+    def forward(stream, s):
+        hop(stream, s - 1, False).wait_recv()
+        if stream in (0, 3):
+            hop(stream, s, True).start()
+        else:
+
+            @pl.when(s < half - 1)
+            def _():
+                hop(stream, s, True).start()
 
     def gather_step(s):
-        hop(0, s - 1, False).wait_recv()
-        hop(0, s, True).start()
-        hop(1, s - 1, False).wait_recv()
+        forward(0, s)
+        forward(1, s)
 
         @pl.when(s < half - 1)
         def _():
-            hop(1, s, True).start()
-
-        hop(2, s - 1, False).wait_recv()
-
-        @pl.when(s < half - 1)
-        def _():
-            hop(2, s, True).start()
-
-        hop(3, s - 1, False).wait_recv()
-        hop(3, s, True).start()
+            stage_a(s + 2)
+
+        select((z + s) % Z)
+        forward(2, s)
+        forward(3, s)
+        select((z + Z - s) % Z)
         use_tokens((z + Z - s) % Z)
         use_tokens((z + s) % Z)
-        use_grads((z + Z - s) % Z)
-        use_grads((z + s) % Z)
+
+        @pl.when(s > 2)
+        def _():
+            pair(s - 2, arrive_x)
 
     each(1, half, gather_step)
+    select((z + half) % Z)
     hop(0, half - 1, False).wait_recv()
+    hop(3, half - 1, False).wait_recv()
     use_tokens((z + half) % Z)
-    hop(3, half - 1, False).wait_recv()
-    use_grads((z + half) % Z)
+
+    arrive_x(z)
+    for s in (half - 2, half - 1, half):
+        pair(s, arrive_x)
 
     gate = acc_gu[:, 0:HP]
     up = acc_gu[:, HP:]
@@ -507,10 +568,16 @@
         result = result + jnp.where(out_lane == k, value, 0.0)
     groute_out[...] = result[0:T, :].astype(BF16)
 
+    each(1, Y, lambda d: y_copy(d, y, y_peer(d)[1]).wait_send())
     for part in range(2):
-        each(1, Y, lambda d, part=part: y_copy(part, d, y, y_peer(d)[1]).wait_send())
-    for part in range(3):
         each(1, NP, lambda d, part=part: x_copy(part, d, x_peer(d)[0], me, x_peer(d)[1]).wait_send())
+    each(1, Z, lambda d: zg_copy(d, z, (w, (z + d) % Z)).wait_send())
+
+    def chunk_sent(chunk):
+        each(1, Y, lambda d: yg_copy(chunk, d, y, y_peer(d)[1]).wait_send())
+        each(1, NP, lambda d: xg_copy(chunk, d, x_peer(d)[0], me, x_peer(d)[1]).wait_send())
+
+    each(0, Z, chunk_sent)
     for stream in range(4):
         n = half if stream in (0, 3) else half - 1
         each(0, n, lambda s, stream=stream: hop(stream, s, True).wait_send())
@@ -548,12 +615,16 @@
     hbm = pl.BlockSpec(memory_space=pl.ANY)
     dma = pltpu.SemaphoreType.DMA
     scratch = [
-        pltpu.VMEM((TP, 2 * F + LANES), BF16),
-        pltpu.VMEM((TOKS, 2 * F + LANES), BF16),
+        pltpu.VMEM((TP, F + LANES), BF16),
+        pltpu.VMEM((TOKS, F + LANES), BF16),
+        pltpu.VMEM((SLOTS, TOKS), BF16),
         pltpu.VMEM((TOKS, SLOTS), BF16),
         pltpu.VMEM((2, SLOTS, LANES), BF16),
         pltpu.VMEM((SLOTS, TOKS), F32),
-        pltpu.VMEM((SLOTS, 2 * F + LANES), BF16),
+        pltpu.VMEM((SLOTS, F + LANES), BF16),
+        pltpu.VMEM((Z, SLOTS, F), BF16),
+        pltpu.VMEM((Z, TP, F), BF16),
+        pltpu.VMEM((Z, TOKS, F), BF16),
         pltpu.VMEM((Z, SLOTS, F), BF16),
         pltpu.VMEM((Z, SLOTS, F), BF16),
         pltpu.VMEM((SLOTS, LANES), BF16),
@@ -574,10 +645,16 @@
         pltpu.VMEM((TOKS, F + LANES), BF16),
         pltpu.VMEM((TOKS, F + LANES), BF16),
         pltpu.VMEM((H, D), BF16),
-        dma((2, Y)),
-        dma((2, Y)),
-        dma((3, NP)),
-        dma((3, NP)),
+        dma((Y,)),
+        dma((Y,)),
+        dma((2, NP)),
+        dma((2, NP)),
+        dma((Z,)),
+        dma((Z,)),
+        dma((Z, Y)),
+        dma((Z, Y)),
+        dma((Z, NP)),
+        dma((Z, NP)),
         dma((4, half)),
         dma((4, half)),
         dma((4, half + 1)),

time: 169 us -> 147 us (0.87)
  Pallas kernels: 162 us -> 139 us
    pallas_call x1, Pallas kernels: 162 us -> 139 us  [body(): pl.pallas_call(functools.partial(kernel, cfg), out_shape=(jax.ShapeDtypeS...]
where the time goes in v2:
time: 147 us; the launch traced here: 146 us
  Pallas kernels  139 us (95%)
  local copies, waits for them, and re-layouts  5.54 us (4%)
    pallas_call x1, Pallas kernels, body(): pl.pallas_call(functools.partial(kernel, cfg), out_shape=(jax.ShapeDtypeS...  139 us
    unnamed x11, local copies, waits for them, and re-layouts  4.93 us

profile of v2, /device:TPU:1, one launch (start us, length us, event | category | flops | bytes accessed | tf_op | source)
XLA Modules:
  0.0 146.1 jit_solution(6224929883491217388)
XLA Ops:
  0.6 0.0 copy-start.2
  0.6 0.7 copy-done.2
  1.3 0.1 copy.11
  1.4 0.0 copy-start.1
  1.4 0.6 pad_convert_fusion.rw_ref
  2.0 0.1 copy-done.1
  2.1 0.1 copy.10
  2.2 0.6 pad.10.ids_ref
  2.8 139.3 %experts.1 = (bf16[24,256]{1,0:T(8,128)(2,1)}, bf16[24,8]{1,0:T(8,128)(2,1)}, bf16[96,4096]{1,0:T(8,128)(2,1)}) custom-call(s32[32,8]{1,0:T(8,128)} %pad.10.ids_ref, f32[32,8]{1,0:T(8,128)} %pad_convert_fusion.rw_ref, bf16[24,256]{1,0:T(8,128)(2,1)} %tok_ref.1, bf16[24,256]{1,0:T(8,128)(2,1)} %grd_ref.1, bf16[96,4096]{1,0:T(8,128)(2,1)} %bitcast.9, ...), custom_call_target="tpu_custom_call" | custom-call | tf_op jit(solution)/shard_map/experts/pallas_call | solution.py:671
  142.1 0.0 copy-start
  142.1 1.3 copy.12
  143.4 0.0 copy-done
  143.4 0.6 copy.15
  144.0 2.1 %copy.16 = bf16[1,96,4096]{2,1,0:T(8,128)(2,1)} copy(bf16[1,96,4096]{2,1,0:T(8,128)(2,1)} %bitcast.8) | data formatting | bytes 1572864
Async XLA Ops:
  0.6 0.7 copy-start.2
  1.4 0.7 copy-start.1
  142.1 1.4 copy-start

commit v3 on v2

--- a/solution.py
+++ b/solution.py
@@ -62,9 +62,16 @@
     acc_gu,
     acc_bp,
     dcat,
-    hidden,
+    hidden_t,
     rs_send,
     rs_recv,
+    bsend,
+    bslot,
+    btok,
+    bcol,
+    bsum,
+    bown,
+    bdone,
     zroute,
     zroute_own,
     rsum,
@@ -90,6 +97,12 @@
     r_rcv,
     z_snd,
     z_rcv,
+    xp_snd,
+    xp_rcv,
+    yp_snd,
+    yp_rcv,
+    zp_snd,
+    zp_rcv,
     xb_snd,
     xb_rcv,
     yb_snd,
@@ -174,8 +187,7 @@
     pack[...] = jnp.zeros_like(pack)
     pack[0:T, 0:F] = tok_ref[...]
     pack[:, F:] = table.astype(BF16)
-    graw[z, 0:T, :] = grd_ref[...]
-    graw[:, T:, :] = jnp.zeros((Z, TP - T, F), BF16)
+    graw[0, 0:T, 0:F] = grd_ref[...]
 
     pl.semaphore_wait(barrier, (Y - 1) + (NP - 1) + (Z - 1))
 
@@ -184,79 +196,82 @@
 
     each(1, Y, lambda d: y_copy(d, y, y_peer(d)[1]).start())
 
-    def zg_copy(d, owner, device):
-        here = graw.at[owner, pl.ds(0, T), :]
-        return remote(here, here, zg_snd.at[d], zg_rcv.at[d], device)
-
-    def yg_copy(chunk, d, owner, device):
-        return remote(
-            graw.at[chunk, pl.ds(0, T), :],
-            gycol.at[chunk, pl.ds(pl.multiple_of(owner * TP, 16), T), :],
-            yg_snd.at[chunk, d],
-            yg_rcv.at[chunk, d],
+    def first(s):
+        return (z + s) % Z
+
+    def second(s):
+        return (z + Z - s + half * (1 - jnp.minimum(s, 1))) % Z
+
+    def zg_copy(d, s, part):
+        return remote(
+            graw.at[0, pl.ds(0, T), pl.ds(0, F)],
+            graw.at[s, pl.ds(0, T), pl.ds(part * F, F)],
+            zg_snd.at[d],
+            zg_rcv.at[d],
+            (w, (z + d) % Z),
+        )
+
+    def yg_copy(s, d, owner, device):
+        return remote(
+            graw.at[s, pl.ds(0, T), :],
+            gycol.at[s, pl.ds(pl.multiple_of(owner * TP, 16), T), :],
+            yg_snd.at[s, d],
+            yg_rcv.at[s, d],
             device,
         )
 
-    def xg_copy(chunk, d, src, dst, device):
-        return remote(
-            gsel.at[chunk, rows(src, PB), :],
-            ggrd.at[chunk, rows(dst, PB), :],
-            xg_snd.at[chunk, d],
-            xg_rcv.at[chunk, d],
+    def xg_copy(s, d, src, dst, device):
+        return remote(
+            gsel.at[s, rows(src, PB), :],
+            ggrd.at[s, rows(dst, PB), :],
+            xg_snd.at[s, d],
+            xg_rcv.at[s, d],
             device,
         )
 
-    each(1, Z, lambda d: zg_copy(d, z, (w, (z + d) % Z)).start())
-
-    def spread_y(chunk):
-        each(1, Y, lambda d: yg_copy(chunk, d, y, y_peer(d)[1]).start())
-        gycol[chunk, rows(y, TP), :] = graw[chunk]
-
-    def arrive_z(chunk):
-        d = (z + Z - chunk) % Z
-        zg_copy(d, chunk, (w, (z + d) % Z)).wait_recv()
-
-    def pair(s, act):
-        act((z + s) % Z)
-
-        @pl.when(s < half)
-        def _():
-            act((z + Z - s) % Z)
+    def zg_start(d):
+        zg_copy(d, d, 1).start()
+        zg_copy(Z - d, d, 0).start()
+
+    each(1, half, zg_start)
+    zg_copy(half, 0, 1).start()
+
+    def spread_y(s):
+        each(1, Y, lambda d: yg_copy(s, d, y, y_peer(d)[1]).start())
+        gycol[s, pl.ds(pl.multiple_of(y * TP, 16), T), :] = graw[s, 0:T, :]
 
     def stage_a(s):
-        def act(chunk):
-            arrive_z(chunk)
-            spread_y(chunk)
-
-        pair(s, act)
-
-    def select(chunk):
+        zg_copy(s, s, 1).wait_recv()
+        zg_copy(Z - s, s, 0).wait_recv()
+        spread_y(s)
+
+    def select(s):
         def one(d):
             yy = (y + Y - d) % Y
-            yg_copy(chunk, d, yy, y_peer(d)[1]).wait_recv()
+            yg_copy(s, d, yy, y_peer(d)[1]).wait_recv()
 
         each(1, Y, one)
-        gsel[chunk] = dot_nn(place_s[...], gycol[chunk]).astype(BF16)
+        gsel[s] = dot_nn(place_s[...], gycol[s]).astype(BF16)
 
         def send(d):
             p, device = x_peer(d)
-            xg_copy(chunk, d, p, me, device).start()
+            xg_copy(s, d, p, me, device).start()
 
         each(1, NP, send)
-        ggrd[chunk, rows(me, PB), :] = gsel[chunk, rows(me, PB), :]
-
-    def arrive_x(chunk):
+        ggrd[s, rows(me, PB), :] = gsel[s, rows(me, PB), :]
+
+    def arrive_x(s):
         def one(d):
             p = (me + NP - d) % NP
-            xg_copy(chunk, d, p, p, x_peer(d)[1]).wait_recv()
+            xg_copy(s, d, p, p, x_peer(d)[1]).wait_recv()
 
         each(1, NP, one)
-        acc_bp[...] += dot_nt(ggrd[chunk], wdn[:, cols(chunk)])
-
-    spread_y(z)
+        acc_bp[...] += dot_nt(ggrd[s, :, 0:F], wdn[:, cols(first(s))])
+        acc_bp[...] += dot_nt(ggrd[s, :, F:], wdn[:, cols(second(s))])
+
     ycol[rows(y, TP), :] = pack[...]
     for j in range(Y):
-        gycol[:, j * TP + T : (j + 1) * TP, :] = jnp.zeros((Z, TP - T, F), BF16)
+        gycol[:, j * TP + T : (j + 1) * TP, :] = jnp.zeros((half, TP - T, 2 * F), BF16)
 
     slot = lax.broadcasted_iota(jnp.int32, (SLOTS, LANES), 0)
     slot_lane = lax.broadcasted_iota(jnp.int32, (SLOTS, LANES), 1)
@@ -338,11 +353,11 @@
     x_wait(0)
     for stream in range(4):
         hop(stream, 0, True).start()
-    select(z)
     stage_a(2)
     for copy in weights:
         copy.wait()
     use_tokens(z)
+    select(1)
 
     key_slot = lax.broadcasted_iota(jnp.int32, (TOKS, SLOTS), 1)
     key_inner = key_slot - PB * steps_of(key_slot, PB, NP)
@@ -366,30 +381,31 @@
         forward(0, s)
         forward(1, s)
 
-        @pl.when(s < half - 1)
+        @pl.when(s < half - 2)
         def _():
             stage_a(s + 2)
 
-        select((z + s) % Z)
+        @pl.when(s == half - 2)
+        def _():
+            zg_copy(half, 0, 1).wait_recv()
+            spread_y(0)
+
         forward(2, s)
         forward(3, s)
-        select((z + Z - s) % Z)
+        select((s + 1) % half)
         use_tokens((z + Z - s) % Z)
         use_tokens((z + s) % Z)
 
-        @pl.when(s > 2)
+        @pl.when(s > 1)
         def _():
-            pair(s - 2, arrive_x)
+            arrive_x(s - 1)
 
     each(1, half, gather_step)
-    select((z + half) % Z)
     hop(0, half - 1, False).wait_recv()
     hop(3, half - 1, False).wait_recv()
     use_tokens((z + half) % Z)
-
-    arrive_x(z)
-    for s in (half - 2, half - 1, half):
-        pair(s, arrive_x)
+    arrive_x(half - 1)
+    arrive_x(0)
 
     gate = acc_gu[:, 0:HP]
     up = acc_gu[:, HP:]
@@ -399,45 +415,122 @@
     active = gate * sig
     slope = sig * (1.0 + gate * (1.0 - sig))
     hid = (active * up).astype(BF16)
-    hidden[...] = hid
+    hidden_t[...] = jnp.transpose(hid.astype(F32)).astype(BF16)
     d_hidden = scale * back
     dcat[:, 0:HP] = (d_hidden * up * slope).astype(BF16)
     dcat[:, HP:] = (d_hidden * active).astype(BF16)
     route = jnp.sum(hid.astype(F32) * back, axis=1, keepdims=True)
 
+    R = SLOTS // 2
+
     def ring(stream, k):
         return remote(
             rs_send.at[stream, k],
             rs_recv.at[stream, k],
             r_snd.at[stream, k],
             r_rcv.at[stream, k],
-            right if stream < 2 else left,
-        )
-
-    def partial(owner):
-        return dot_nn(dcat[...], wgu[:, cols(owner)])
-
-    def push(stream, k, value, add):
+            right if stream % 2 == 0 else left,
+        )
+
+    def partial(owner, part):
+        lanes = pl.ds(pl.multiple_of(owner * F + part * A, LANES), A)
+        return dot_nn(dcat[...], wgu[:, lanes])
+
+    def push(stream, k, values, add):
+        value = values[(stream // 2) * R : (stream // 2 + 1) * R]
         if add:
             ring(stream, k + 1).wait_recv()
             value = value + rs_recv[stream, k + 1].astype(F32)
         rs_send[stream, k] = value.astype(BF16)
         ring(stream, k).start()
 
-    def down(chunk):
-        scaled = (jnp.concatenate([scale_ref()] * (F // LANES), axis=1) * ggrd[chunk].astype(F32)).astype(BF16)
-        gdown[:, cols(chunk)] = dot_tn(hidden[...], scaled)[0:H, :].astype(BF16)
-
-    def scale_ref():
-        return gain[...].astype(F32)
-
-    far = partial((z + half) % Z)
-    push(0, half, far[:, 0:A], False)
-    push(3, half, far[:, A:], False)
-    to_right = partial((z + half - 1) % Z)
-    to_left = partial((z + Z - half + 1) % Z)
-    push(1, half - 1, to_right[:, A:], False)
-    push(2, half - 1, to_left[:, 0:A], False)
+    def down(s, part):
+        owner = second(s) if part else first(s)
+        scale = gain[...].astype(F32)
+        rows_of = ggrd[s, :, part * F : (part + 1) * F].astype(F32)
+        scaled = (jnp.concatenate([scale] * (F // LANES), axis=1) * rows_of).astype(BF16)
+        gdown[:, cols(owner)] = dot_nn(hidden_t[...], scaled)[0:H, :].astype(BF16)
+
+    def xp_copy(s, d, src, dst, device):
+        return remote(
+            bsend.at[s, rows(src, PB), :],
+            bslot.at[s, rows(dst, PB), :],
+            xp_snd.at[s, d],
+            xp_rcv.at[s, d],
+            device,
+        )
+
+    def yp_copy(s, d, src, dst, device):
+        return remote(
+            btok.at[s, pl.ds(pl.multiple_of(src * TP, 16), T), :],
+            bcol.at[s, pl.ds(pl.multiple_of(dst * TP, 16), T), :],
+            yp_snd.at[s, d],
+            yp_rcv.at[s, d],
+            device,
+        )
+
+    def zp_copy(s, part, d):
+        return remote(
+            bsum.at[s, pl.ds(0, T), pl.ds(part * A, A)],
+            bdone.at[d, pl.ds(0, T), :],
+            zp_snd.at[d],
+            zp_rcv.at[d],
+            (w, (z + d) % Z),
+        )
+
+    def back_x(s):
+        bsend[s, :, 0:A] = partial(first(s), 1).astype(BF16)
+        bsend[s, :, A:] = partial(second(s), 1).astype(BF16)
+
+        def send(d):
+            p, device = x_peer(d)
+            xp_copy(s, d, p, me, device).start()
+
+        each(1, NP, send)
+        bslot[s, rows(me, PB), :] = bsend[s, rows(me, PB), :]
+
+    def back_y(s):
+        def one(d):
+            p = (me + NP - d) % NP
+            xp_copy(s, d, p, p, x_peer(d)[1]).wait_recv()
+
+        each(1, NP, one)
+        btok[s] = dot_nn(place_t[...], bslot[s]).astype(BF16)
+
+        def send(d):
+            yy, device = y_peer(d)
+            yp_copy(s, d, yy, y, device).start()
+
+        each(1, Y, send)
+        here = pl.ds(pl.multiple_of(y * TP, 16), T)
+        bcol[s, here, :] = btok[s, here, :]
+
+    def back_z(s):
+        def one(d):
+            yy = (y + Y - d) % Y
+            yp_copy(s, d, yy, yy, y_peer(d)[1]).wait_recv()
+
+        each(1, Y, one)
+        total = bcol[s, 0:T, :].astype(F32)
+        for j in range(1, Y):
+            total = total + bcol[s, j * TP : j * TP + T, :].astype(F32)
+        bsum[s, 0:T, :] = total.astype(BF16)
+        return total
+
+    def back_z_pair(s):
+        back_z(s)
+        zp_copy(s, 0, s).start()
+        zp_copy(s, 1, Z - s).start()
+
+    far = partial((z + half) % Z, 0)
+    push(0, half, far, False)
+    push(3, half, far, False)
+    back_x(0)
+    to_right = partial((z + half - 1) % Z, 0)
+    to_left = partial((z + Z - half + 1) % Z, 0)
+    push(2, half - 1, to_right, False)
+    push(1, half - 1, to_left, False)
+    back_x(half - 1)
 
     rt_row = lax.broadcasted_iota(jnp.int32, (SLOTS, LANES), 0)
     rt_inner = rt_row - PB * steps_of(rt_row, PB, NP)
@@ -453,31 +546,35 @@
 
     each(1, Z, lambda d: z_copy(d, d, (w, (z + d) % Z)).start())
 
-    push(0, half - 1, to_right[:, 0:A], True)
-    push(3, half - 1, to_left[:, A:], True)
-    for chunk in range(2):
-        down(chunk)
-
-    def reduce_step(i):
+    push(0, half - 1, to_right, True)
+    push(3, half - 1, to_left, True)
+
+    def reduce_step(k):
+        to_right = partial((z + k) % Z, 0)
+        to_left = partial((z + Z - k) % Z, 0)
+        push(0, k, to_right, True)
+        push(1, k, to_left, True)
+        push(2, k, to_right, True)
+        push(3, k, to_left, True)
+
+    def reduce_loop(i):
         k = half - 1 - i
-        to_right = partial((z + k) % Z)
-        to_left = partial((z + Z - k) % Z)
-        push(0, k, to_right[:, 0:A], True)
-        push(3, k, to_left[:, A:], True)
-        push(1, k, to_right[:, A:], True)
-        push(2, k, to_left[:, 0:A], True)
-        per = -(-(Z - 2) // (half - 2))
-        for j in range(per):
-            chunk = 2 + (i - 1) * per + j
-
-            @pl.when(chunk < Z)
-            def _():
-                down(chunk)
-
-    each(1, half - 1, reduce_step)
-    out_copy = pltpu.make_async_copy(gdown, gdown_out, o_sem)
-    out_copy.start()
-
+        reduce_step(k)
+
+        @pl.when(k > 1)
+        def _():
+            back_x(k - 1)
+
+        back_y((k + 2) % half)
+
+        @pl.when(k < half - 4)
+        def _():
+            back_z_pair(k + 4)
+
+        down(k, 0)
+
+    back_x(half - 2)
+    each(1, half - 1, reduce_loop)
     each(1, Z, lambda d: z_copy(d, d, (w, (z + d) % Z)).wait_recv())
     total = zroute_own[...]
     for d in range(1, Z):
@@ -512,15 +609,22 @@
     xb_start(0)
     xroute[me] = rsum[...]
 
-    own = partial(z)
-    for lanes, streams in ((slice(0, A), (0, 2)), (slice(A, F), (1, 3))):
-        value = own[:, lanes]
-        for stream in streams:
+    own = partial(z, 0)
+    for part in range(2):
+        here = slice(part * R, (part + 1) * R)
+        value = own[here]
+        for stream in (2 * part, 2 * part + 1):
             ring(stream, 1).wait_recv()
             value = value + rs_recv[stream, 1].astype(F32)
-        cgrad[:, lanes] = value.astype(BF16)
+        cgrad[here, :] = value.astype(BF16)
     xb_start(1)
     xback[rows(me, PB), :] = cgrad[rows(me, PB), :]
+    back_y(2)
+    back_z_pair(4)
+    back_y(1)
+    bown[...] = back_z(0)[:, 0:A]
+    zp_copy(0, 1, half).start()
+    back_z_pair(3)
 
     xb_wait(0)
     sub = lax.broadcasted_iota(jnp.int32, (NP, 8, LANES), 1)
@@ -533,10 +637,10 @@
     slot_peer = steps_of(lax.broadcasted_iota(jnp.int32, (NP, SLOTS), 1), PB, NP)
     values = jnp.sum(jnp.where(from_peer == slot_peer, wide_rows, 0.0), axis=0, keepdims=True)
     routed = (place_t[...].astype(F32) * values).astype(BF16)
-    yback_send[:, F:] = dot_nn(routed, emat[0]).astype(BF16)
+    yback_send[:, A:] = dot_nn(routed, emat[0]).astype(BF16)
 
     xb_wait(1)
-    yback_send[:, 0:F] = dot_nn(place_t[...], xback[...]).astype(BF16)
+    yback_send[:, 0:A] = dot_nn(place_t[...], xback[...]).astype(BF16)
 
     def yb_copy(d, src, dst, device):
         return remote(
@@ -549,17 +653,25 @@
 
     each(1, Y, yb_start)
     yback[rows(y, TP), :] = yback_send[rows(y, TP), :]
+    back_z_pair(2)
+    back_z_pair(1)
+    each(1, half - 1, lambda s: down(s, 1))
+    for s in (0, half - 1):
+        down(s, 0)
+        down(s, 1)
+    out_copy = pltpu.make_async_copy(gdown, gdown_out, o_sem)
+    out_copy.start()
 
     def yb_wait(d):
         yy = (y + Y - d) % Y
         yb_copy(d, yy, yy, y_peer(d)[1]).wait_recv()
 
     each(1, Y, yb_wait)
-    final = jnp.zeros((TP, F + LANES), F32)
+    final = jnp.zeros((TP, A + LANES), F32)
     for j in range(Y):
         final = final + yback[j * TP : (j + 1) * TP, :].astype(F32)
-    gtok_out[...] = final[0:T, 0:F].astype(BF16)
-    per_expert = final[:, F:]
+    gtok_out[:, 0:A] = final[0:T, 0:A].astype(BF16)
+    per_expert = final[:, A:]
     out_lane = lax.broadcasted_iota(jnp.int32, (TP, TOP), 1)
     result = jnp.zeros((TP, TOP), F32)
     for k in range(TOP):
@@ -568,16 +680,28 @@
         result = result + jnp.where(out_lane == k, value, 0.0)
     groute_out[...] = result[0:T, :].astype(BF16)
 
+    def done(d):
+        zp_copy(0, 0, d).wait_recv()
+
+    each(1, Z, done)
+    rest = bown[...]
+    for d in range(1, Z):
+        rest = rest + bdone[d, 0:T, :].astype(F32)
+    gtok_out[:, A:] = rest.astype(BF16)
+
     each(1, Y, lambda d: y_copy(d, y, y_peer(d)[1]).wait_send())
     for part in range(2):
         each(1, NP, lambda d, part=part: x_copy(part, d, x_peer(d)[0], me, x_peer(d)[1]).wait_send())
-    each(1, Z, lambda d: zg_copy(d, z, (w, (z + d) % Z)).wait_send())
+    each(1, Z, lambda d: zg_copy(d, 0, 1).wait_send())
 
     def chunk_sent(chunk):
         each(1, Y, lambda d: yg_copy(chunk, d, y, y_peer(d)[1]).wait_send())
         each(1, NP, lambda d: xg_copy(chunk, d, x_peer(d)[0], me, x_peer(d)[1]).wait_send())
-
-    each(0, Z, chunk_sent)
+        each(1, NP, lambda d: xp_copy(chunk, d, x_peer(d)[0], me, x_peer(d)[1]).wait_send())
+        each(1, Y, lambda d: yp_copy(chunk, d, y_peer(d)[0], y, y_peer(d)[1]).wait_send())
+
+    each(0, half, chunk_sent)
+    each(1, Z, lambda d: zp_copy(0, 0, d).wait_send())
     for stream in range(4):
         n = half if stream in (0, 3) else half - 1
         each(0, n, lambda s, stream=stream: hop(stream, s, True).wait_send())
@@ -623,27 +747,34 @@
         pltpu.VMEM((SLOTS, TOKS), F32),
         pltpu.VMEM((SLOTS, F + LANES), BF16),
         pltpu.VMEM((Z, SLOTS, F), BF16),
-        pltpu.VMEM((Z, TP, F), BF16),
-        pltpu.VMEM((Z, TOKS, F), BF16),
-        pltpu.VMEM((Z, SLOTS, F), BF16),
-        pltpu.VMEM((Z, SLOTS, F), BF16),
+        pltpu.VMEM((half, TP, 2 * F), BF16),
+        pltpu.VMEM((half, TOKS, 2 * F), BF16),
+        pltpu.VMEM((half, SLOTS, 2 * F), BF16),
+        pltpu.VMEM((half, SLOTS, 2 * F), BF16),
         pltpu.VMEM((SLOTS, LANES), BF16),
         pltpu.VMEM((2 * HP, D), BF16),
         pltpu.VMEM((HP, D), BF16),
         pltpu.VMEM((SLOTS, 2 * HP), F32),
         pltpu.VMEM((SLOTS, HP), F32),
         pltpu.VMEM((SLOTS, 2 * HP), BF16),
-        pltpu.VMEM((SLOTS, HP), BF16),
-        pltpu.VMEM((4, half + 1, SLOTS, A), BF16),
-        pltpu.VMEM((4, half + 1, SLOTS, A), BF16),
+        pltpu.VMEM((HP, SLOTS), BF16),
+        pltpu.VMEM((4, half + 1, SLOTS // 2, A), BF16),
+        pltpu.VMEM((4, half + 1, SLOTS // 2, A), BF16),
+        pltpu.VMEM((half, SLOTS, F), BF16),
+        pltpu.VMEM((half, SLOTS, F), BF16),
+        pltpu.VMEM((half, TOKS, F), BF16),
+        pltpu.VMEM((half, TOKS, F), BF16),
+        pltpu.VMEM((half, TP, F), BF16),
+        pltpu.VMEM((T, A), F32),
+        pltpu.VMEM((Z, TP, A), BF16),
         pltpu.VMEM((Z, 8, LANES), F32),
         pltpu.VMEM((8, LANES), F32),
         pltpu.VMEM((8, LANES), F32),
         pltpu.VMEM((NP, 8, LANES), F32),
-        pltpu.VMEM((SLOTS, F), BF16),
-        pltpu.VMEM((SLOTS, F), BF16),
-        pltpu.VMEM((TOKS, F + LANES), BF16),
-        pltpu.VMEM((TOKS, F + LANES), BF16),
+        pltpu.VMEM((SLOTS, A), BF16),
+        pltpu.VMEM((SLOTS, A), BF16),
+        pltpu.VMEM((TOKS, A + LANES), BF16),
+        pltpu.VMEM((TOKS, A + LANES), BF16),
         pltpu.VMEM((H, D), BF16),
         dma((Y,)),
         dma((Y,)),
@@ -651,14 +782,20 @@
         dma((2, NP)),
         dma((Z,)),
         dma((Z,)),
-        dma((Z, Y)),
-        dma((Z, Y)),
-        dma((Z, NP)),
-        dma((Z, NP)),
+        dma((half, Y)),
+        dma((half, Y)),
+        dma((half, NP)),
+        dma((half, NP)),
         dma((4, half)),
         dma((4, half)),
         dma((4, half + 1)),
         dma((4, half + 1)),
+        dma((Z,)),
+        dma((Z,)),
+        dma((half, NP)),
+        dma((half, NP)),
+        dma((half, Y)),
+        dma((half, Y)),
         dma((Z,)),
         dma((Z,)),
         dma((2, NP)),

time: 147 us -> 139 us (0.946)
  Pallas kernels: 139 us -> 132 us
    pallas_call x1, Pallas kernels: 139 us -> 132 us  [body(): pl.pallas_call(functools.partial(kernel, cfg), out_shape=(jax.ShapeDtypeS...]
where the time goes in v3:
time: 139 us
  Pallas kernels  132 us (95%)
  local copies, waits for them, and re-layouts  5.54 us (4%)
    pallas_call x1, Pallas kernels, body(): pl.pallas_call(functools.partial(kernel, cfg), out_shape=(jax.ShapeDtypeS...  132 us
    unnamed x11, local copies, waits for them, and re-layouts  4.93 us

profile of v3, /device:TPU:1, one launch (start us, length us, event | category | flops | bytes accessed | tf_op | source)
XLA Modules:
  0.0 138.9 jit_solution(6005303383027740050)
XLA Ops:
  0.6 0.0 copy-start.2
  0.6 0.7 copy-done.2
  1.3 0.1 copy.11
  1.4 0.0 copy-start.1
  1.4 0.6 pad_convert_fusion.rw_ref
  2.0 0.1 copy-done.1
  2.1 0.1 copy.10
  2.2 0.6 pad.10.ids_ref
  2.8 132.1 %experts.1 = (bf16[24,256]{1,0:T(8,128)(2,1)}, bf16[24,8]{1,0:T(8,128)(2,1)}, bf16[96,4096]{1,0:T(8,128)(2,1)}) custom-call(s32[32,8]{1,0:T(8,128)} %pad.10.ids_ref, f32[32,8]{1,0:T(8,128)} %pad_convert_fusion.rw_ref, bf16[24,256]{1,0:T(8,128)(2,1)} %tok_ref.1, bf16[24,256]{1,0:T(8,128)(2,1)} %grd_ref.1, bf16[96,4096]{1,0:T(8,128)(2,1)} %bitcast.9, ...), custom_call_target="tpu_custom_call" | custom-call | tf_op jit(solution)/shard_map/experts/pallas_call | solution.py:808
  134.9 0.0 copy-start
  134.9 1.3 copy.12
  136.2 0.0 copy-done
  136.2 0.6 copy.15
  136.8 2.1 %copy.16 = bf16[1,96,4096]{2,1,0:T(8,128)(2,1)} copy(bf16[1,96,4096]{2,1,0:T(8,128)(2,1)} %bitcast.8) | data formatting | bytes 1572864
Async XLA Ops:
  0.6 0.7 copy-start.2
  1.4 0.7 copy-start.1
  134.9 1.4 copy-start
